TPU v7x, 512 devices: a whole 4x4x16 slice. The times are simulated.
512 devices in a mesh: row: 64 (over z_hi, x, y), col: 8 (over z_lo, core).
Axes of the slice: x: 4, y: 4, z: 16 (z_hi: 4, z_lo: 4; z = z_hi * 4 + z_lo), core: 2. Of those that a mesh axis runs over, the one named last changes fastest.
Arguments:
- tensor: float32 [8, 8192, 8192], P(None, 'row', 'col'), may hold values from -0.8 to 0.8
- factor_a: float32 [8192, 256], P(('row', 'col')), may hold values from -0.0625 to 0.0625
- factor_bt: float32 [256, 8192], P('row', 'col'), may hold values from -0.0625 to 0.0625
- factor_c: float32 [8, 256], replicated, may hold values from -6 to 6
Outputs:
- grad_a: float32 [8192, 256], P(('row', 'col'))
- grad_bt: float32 [256, 8192], P('row', 'col')
- grad_c: float32 [8, 256], replicated
All inputs are finite; a program needn't handle non-finite values.
Results may differ from a plain program's by a relative error of at most 0.0001.
Values sent between devices are 32-bit elements; how exact they have to be, the bound alone decides.
A program may use at most 64 MiB of HBM per device.

v0:
```python
import jax
import jax.numpy as jnp
from jax import lax
from jax.sharding import PartitionSpec as P


def local(tensor, factor_a, factor_bt, factor_c):
    highest = lax.Precision.HIGHEST
    rank_rows = factor_bt.shape[0]
    block_a = lax.all_gather(factor_a, "col", axis=0, tiled=True)
    gram_c = jnp.dot(factor_c.T, factor_c, precision=highest)
    weighted = block_a[None, :, :] * factor_c[:, None, :]
    block_bt = lax.all_gather(factor_bt, "row", axis=0, tiled=True)
    mttkrp_bt = lax.psum_scatter(
        jnp.einsum("kir,kij->rj", weighted, tensor, precision=highest),
        "row",
        scatter_dimension=0,
        tiled=True,
    )
    contracted = jnp.einsum("kij,rj->kir", tensor, block_bt, precision=highest)
    partial_a = jnp.sum(contracted * factor_c[:, None, :], axis=0)
    partial_c = jnp.sum(contracted * block_a[None, :, :], axis=1)
    mttkrp_a = lax.psum_scatter(partial_a, "col", scatter_dimension=0, tiled=True)
    mttkrp_c = lax.psum(partial_c, ("row", "col"))
    local_gram_a = jnp.dot(factor_a.T, factor_a, precision=highest)
    gram_a = lax.psum(local_gram_a, ("row", "col"))
    gram_b = lax.psum(jnp.dot(block_bt, block_bt.T, precision=highest), "col")
    grad_a = jnp.dot(factor_a, gram_b * gram_c, precision=highest) - mttkrp_a
    h_rows = lax.dynamic_slice_in_dim(
        gram_a * gram_c, lax.axis_index("row") * rank_rows, rank_rows, 0
    )
    grad_bt = jnp.dot(h_rows, block_bt, precision=highest) - mttkrp_bt
    grad_c = jnp.dot(factor_c, gram_a * gram_b, precision=highest) - mttkrp_c
    return (grad_a, grad_bt, grad_c)


def solution(mesh):
    in_specs = (P(None, "row", "col"), P(("row", "col"), None), P("row", "col"), P())
    out_specs = (P(("row", "col"), None), P("row", "col"), P())
    return jax.shard_map(local, mesh=mesh, in_specs=in_specs, out_specs=out_specs, check_vma=False)
```

profile of v0, /device:TPU:1, one launch (start us, length us, event | category | flops | bytes accessed | tf_op | source)
XLA Modules:
  0.0 1438.0 jit_solution(11810171701839936095)
XLA Ops:
  8.0 0.0 all-gather.3.cloned.1.call-start
  8.0 0.7 all-gather.3.cloned.1.call-update
  8.7 0.0 all-reduce.7.cloned.1.call-start
  8.8 1.9 fusion.11
  10.7 0.0 all-reduce.7.cloned.1.call-update
  10.7 0.0 all-reduce.9.cloned.1.call-start
  10.8 20.9 %all_gather.7 = f32[128,256]{1,0:T(8,128)S(1)} all-gather(f32[16,256]{1,0:T(8,128)} %param.5), channel_id=1, replica_groups=mesh['row'=64,'col'=8] {'col'}, dimensions={0}, use_global_device_ids=true | all-gather | bytes 147456 | tf_op jit(solution)/shard_map/all_gather | solution.py:10
  31.6 0.0 copy-start.2
  31.7 6.8 convolution_bitcast_fusion
  38.5 0.0 all-reduce.9.cloned.1.call-update
  38.5 0.0 reduce-scatter.2.cloned.1.call-start
  38.5 83.1 %all-gather.3.cloned.1.call-done = f32[64,4,1024]{2,1,0:T(4,128)} async-done(((f32[1,4,1024]{2,1,0:T(4,128)}), f32[64,4,1024]{2,1,0:T(4,128)}) %all-gather.3.cloned.1.call-update) | async-done | bytes 1048592 | tf_op jit(solution)/shard_map/all_gather | solution.py:13
  121.6 0.0 copy-start
  121.6 1.7 reshape.10
  123.3 0.0 copy-done.2
  123.3 6.3 multiply_reduce_fusion
  129.7 0.0 reduce-scatter.2.cloned.1.call-update
  129.7 0.0 all-reduce.5.cloned.1.call-start
  129.7 0.0 copy-done
  129.8 0.4 reshape.9
  130.1 1.7 fusion.9
  131.9 0.0 all-reduce.5.cloned.1.call-update
  131.9 0.4 fusion.10
  132.3 1.3 dynamic-slice
  134.2 103.7 %psum.23 = f32[8,256]{1,0:T(8,128)S(1)} all-reduce(f32[8,256]{1,0:T(8,128)S(1)} %get-tuple-element.3), channel_id=1, replica_groups=mesh['row'=64,'col'=8] {'row','col'}, use_global_device_ids=true, to_apply=%region_6.0 | all-reduce | flops 2048 | bytes 16384 | tf_op jit(solution)/shard_map/psum | solution.py:24
  238.0 253.3 %all-reduce.7.cloned.1.call-done = f32[256,256]{1,0:T(8,128)} async-done(((f32[256,256]{1,0:T(8,128)}), f32[256,256]{1,0:T(8,128)}) %all-reduce.7.cloned.1.call-update) | async-done | bytes 262160 | tf_op jit(solution)/shard_map/psum | solution.py:26
  491.3 810.8 %all-reduce.9.cloned.1.call-done = f32[256,1024]{1,0:T(8,128)} async-done(((f32[256,1024]{1,0:T(8,128)}), f32[256,1024]{1,0:T(8,128)}) %all-reduce.9.cloned.1.call-update) | async-done | bytes 1048592
  1302.1 2.0 convolution_subtract_fusion
  1304.1 122.6 %all-reduce.5.cloned.1.call-done = f32[256,256]{1,0:T(8,128)} async-done(((f32[256,256]{1,0:T(8,128)}), f32[256,256]{1,0:T(8,128)}) %all-reduce.5.cloned.1.call-update) | async-done | bytes 262160 | tf_op jit(solution)/shard_map/psum | solution.py:27
  1426.7 0.0 copy-done.1
  1426.7 1.8 fusion
  1428.5 1.9 fusion.1
  (2 shorter events, 0.0 us)
Async XLA Ops:
  8.0 113.6 %all-gather.3.cloned.1.call-start = ((), (), s32[]{:S(2)}) async-start(), calls=%async_computation.4 | async-start | bytes 1064960 | tf_op jit(solution)/shard_map/all_gather | solution.py:13
  8.7 482.6 %all-reduce.7.cloned.1.call-start = ((), (), s32[]{:S(2)}) async-start(), calls=%async_computation.3 | async-start | bytes 524288 | tf_op jit(solution)/shard_map/psum | solution.py:26
  10.7 1291.3 %all-reduce.9.cloned.1.call-start = ((), (), s32[]{:S(2)}) async-start(), calls=%async_computation.5 | async-start | bytes 2097152
  31.6 91.7 %copy-start.2 = (f32[8,256]{1,0:T(8,128)S(1)}, f32[8,256]{1,0:T(8,128)}, u32[]{:S(2)}) copy-start(f32[8,256]{1,0:T(8,128)} %param.7) | copy-start | bytes 24580
  38.5 1265.6 %reduce-scatter.2.cloned.1.call-start = ((), (), s32[]{:S(2)}) async-start(), calls=%async_computation.2 | async-start | bytes 147456 | tf_op jit(solution)/shard_map/reduce_scatter | solution.py:23
  121.6 8.1 copy-start
  129.7 1297.0 %copy-start.1 = (f32[16,256]{1,0:T(8,128)S(1)}, f32[16,256]{1,0:T(8,128)}, u32[]{:S(2)}) copy-start(f32[16,256]{1,0:T(8,128)} %param.5) | copy-start | bytes 49156
  129.7 1297.0 %all-reduce.5.cloned.1.call-start = ((), (), s32[]{:S(2)}) async-start(), calls=%async_computation.1 | async-start | bytes 524288 | tf_op jit(solution)/shard_map/psum | solution.py:27
Sparse Core Ops, SparseCore 0:
  13.0 108.6 all-gather.2
  129.8 34.5 reduce-scatter.1
Sparse Core Ops, SparseCore 1:
  14.7 476.6 all-reduce.6
  494.1 807.9 all-reduce.8
  1304.8 121.8 all-reduce.4
where the time goes:
time: 1440 us
  waiting for transfers between devices  1270 us (88%)
  blocking collectives  125 us (9%)
  matrix products  22.9 us (2%)
  between operations  16.4 us (1%)
    unnamed x6, waiting for transfers between devices  812 us
    psum x1, waiting for transfers between devices, local(): gram_a = lax.psum(local_gram_a, ('row', 'col'))  253 us
    psum x1, waiting for transfers between devices, local(): gram_b = lax.psum(jnp.dot(block_bt, block_bt.T, precision=highest), 'col')  123 us
    psum x1, blocking collectives, local(): mttkrp_c = lax.psum(partial_c, ('row', 'col'))  104 us
    all_gather x1, waiting for transfers between devices, local(): block_bt = lax.all_gather(factor_bt, 'row', axis=0, tiled=True)  83.1 us
  transfers between devices with their start and end apart: 5, of which 4 were waited for; matrix products, arithmetic and copies ran while one was open for 2% of the time, Pallas kernels for 0%

commit v1 on v0

v1 whole, which is shorter than its diff:
```python
import jax
import jax.numpy as jnp
from jax import lax
from jax.experimental import pallas as pl
from jax.experimental.pallas import tpu as pltpu
from jax.sharding import PartitionSpec as P

MESH = pl.DeviceIdType.MESH
F32, BF16 = jnp.float32, jnp.bfloat16
NSEM = 160
NN = (((1,), (0,)), ((), ()))
NT = (((1,), (1,)), ((), ()))


def split(v):
    hi = v.astype(BF16)
    return hi, (v - hi.astype(F32)).astype(BF16)


def dot3(a, b, dims):
    def one(u, v):
        return lax.dot_general(u, v, dims, preferred_element_type=F32)

    return one(a[0], b[0]) + (one(a[0], b[1]) + one(a[1], b[0]))


def kernel(
    t_hbm, a_ref, bt_ref, c_ref,
    ga_out, gbt_out, gc_out,
    tf, thi, tlo, whi, wlo, m1, ab, bg, btn, bhi, blo, hm, gam, gcm, gbm,
    gr, r1, r2, z1, z2, pa, pcore, psum, pz, pck, cown, ccore, cx, cy, cz, ch, cf,
    ct, ssem, rsem, lsem,
):
    row, col = lax.axis_index("row"), lax.axis_index("col")
    zh, x, y = row // 16, (row // 4) % 4, row % 4
    zl, core = col // 2, col % 2
    other = 1 - core

    def at_row(h, i, j):
        return (h * 16 + i * 4 + j, col)

    def xp(d):
        return at_row(zh, (x + d) % 4, y)

    def yp(d):
        return at_row(zh, x, (y + d) % 4)

    def zp(d):
        return at_row((zh + d) % 4, x, y)

    def lp(d):
        return (row, ((zl + d) % 4) * 2 + core)

    twin = (row, zl * 2 + other)
    sent = []

    def send(src, dst, device):
        k = len(sent)
        copy = pltpu.make_async_remote_copy(
            src_ref=src, dst_ref=dst, send_sem=ssem.at[k], recv_sem=rsem.at[k],
            device_id=device, device_id_type=MESH,
        )
        copy.start()
        sent.append(copy)
        return copy

    def arrive(copies):
        for copy in copies:
            copy.wait_recv()

    load_t = pltpu.make_async_copy(t_hbm, tf, lsem.at[0])
    load_t.start()
    own_bt = pltpu.make_async_copy(bt_ref, bg.at[zh, x, y], lsem.at[1])
    own_bt.start()
    own_a = pltpu.make_async_copy(a_ref, ab.at[zl, core], lsem.at[2])
    own_a.start()

    barrier = pltpu.get_barrier_semaphore()
    peers = [f(d) for f in (xp, yp, lp) for d in (1, 2, 3)] + [zp(1), zp(3), twin]
    for device in peers:
        pl.semaphore_signal(barrier, inc=1, device_id=device, device_id_type=MESH)
    pl.semaphore_wait(barrier, len(peers))

    def stage1(w, slot):
        return [send(slot.at[0], bg.at[w, x, y, 0], xp(d)) for d in (1, 2, 3)] + [
            send(slot.at[1], bg.at[w, x, y, 1], yp(d)) for d in (1, 2, 3)
        ]

    def stage2(w):
        return [
            send(bg.at[w, :, y, 0], bg.at[w, :, y, 0], yp(d)) for d in (1, 2, 3)
        ] + [send(bg.at[w, x, :, 1], bg.at[w, x, :, 1], xp(d)) for d in (1, 2, 3)]

    up, down, far = (zh + 1) % 4, (zh + 3) % 4, (zh + 2) % 4
    mine = bg.at[zh, x, y]
    z_up = send(bt_ref, mine, zp(1))
    z_down = send(bt_ref, mine, zp(3))
    a_line = [send(a_ref, ab.at[zl, core], lp(d)) for d in (1, 2, 3)]
    own1 = stage1(zh, bt_ref)
    own_bt.wait()
    own_a.wait()

    load_t.wait()

    def split_t(k, _):
        hi, lo = split(tf[k])
        at = pl.ds(pl.multiple_of(k * 128, 128), 128)
        thi[at, :] = hi
        tlo[at, :] = lo
        return 0

    lax.fori_loop(0, 4, split_t, 0)
    arrive(own1)
    own2 = stage2(zh)
    arrive(a_line)
    a_twin = send(ab.at[:, core], ab.at[:, core], twin)
    z_up.wait_recv()
    on_up = send(bg.at[down, x, y, 0], bg.at[down, x, y, 0], zp(1))
    down1 = stage1(down, bg.at[down, x, y])
    z_down.wait_recv()
    on_down = send(bg.at[up, x, y, 1], bg.at[up, x, y, 1], zp(3))
    up1 = stage1(up, bg.at[up, x, y])
    lax.fori_loop(4, 8, split_t, 0)

    a_twin.wait_recv()
    block_a = ab[...].reshape(128, 256)
    c_all = c_ref[...]
    a_t = jnp.transpose(block_a)
    ct[...] = jnp.transpose(jnp.concatenate([c_all, jnp.zeros((120, 256), F32)], 0))
    c_t = split(ct[...])
    gcm[...] = dot3(c_t, c_t, NT)
    a_t_split = split(a_t)
    gam[...] = dot3(a_t_split, a_t_split, NT)
    for k in range(8):
        hi, lo = split(a_t * ct[:, k : k + 1])
        whi[:, k * 128 : (k + 1) * 128] = hi
        wlo[:, k * 128 : (k + 1) * 128] = lo

    def first(j, _):
        at = pl.ds(pl.multiple_of(j * 256, 256), 256)
        m1[:, at] = dot3((whi[...], wlo[...]), (thi[:, at], tlo[:, at]), NN)
        return 0

    arrive([on_up, on_down])
    far1 = stage1(far, bg.at[far, x, y])
    arrive(down1)
    down2 = stage2(down)
    arrive(up1)
    up2 = stage2(up)
    lax.fori_loop(0, 2, first, 0)
    arrive(far1)
    far2 = stage2(far)
    h_split = split(gam[...] * gcm[...])
    hm[0], hm[1] = h_split
    lax.fori_loop(2, 4, first, 0)
    arrive(own2 + down2 + up2 + far2)

    bg2 = bg.reshape(2048, 128)
    for j in range(8):
        for q in range(4):
            btn[j, pl.ds(q, 64, stride=4), :] = bg2[pl.ds(j * 4 + q, 64, stride=32), :]
        hi, lo = split(btn[j])
        bhi[:, j * 128 : (j + 1) * 128] = hi
        blo[:, j * 128 : (j + 1) * 128] = lo

    b_split = (bhi[...], blo[...])
    gbm[...] = dot3(b_split, b_split, NT)

    pa[...] = jnp.zeros_like(pa)

    def second(m, _):
        at = pl.ds(pl.multiple_of(m * 512, 512), 512)
        part = dot3((thi[at, :], tlo[at, :]), (bhi[...], blo[...]), NT)
        rows_a = ab[...].reshape(128, 256)
        acc = pa[...].reshape(128, 256)
        for k in range(4):
            one = part[k * 128 : (k + 1) * 128]
            acc = acc + one * c_ref[pl.ds(m * 4 + k, 1), :]
            pck[pl.ds(m * 4 + k, 1), :] = jnp.sum(one * rows_a, axis=0, keepdims=True)
        pa[...] = acc.reshape(4, 2, 16, 256)
        return 0

    lax.fori_loop(0, 2, second, 0)
    c_part = dot3(split(c_ref[...]), split(gam[...] * gbm[...]), NN) - pck[...]
    cown[0] = c_part[:, :128]
    cown[1] = c_part[:, 128:]
    c1 = send(cown.at[other], ccore, twin)

    def third(j, _):
        at = pl.ds(pl.multiple_of(j * 256, 256), 256)
        got = dot3((hm[0], hm[1]), (bhi[:, at], blo[:, at]), NN) - m1[:, at]
        btn[2 * j] = got[:, :128]
        btn[2 * j + 1] = got[:, 128:]
        return 0

    lax.fori_loop(0, 4, third, 0)
    gr2 = gr.reshape(2048, 128)
    for j in range(8):
        for q in range(4):
            gr2[pl.ds(j * 4 + q, 64, stride=32), :] = btn[j, pl.ds(q, 64, stride=4), :]

    def scatter1(n, w):
        return [
            send(gr.at[w, :, (y + d) % 4, 0], r1.at[n, 0, d - 1], yp(d))
            for d in (1, 2, 3)
        ] + [
            send(gr.at[w, (x + d) % 4, :, 1], r1.at[n, 1, d - 1], xp(d))
            for d in (1, 2, 3)
        ]

    def scatter2(n, w, copies):
        arrive(copies)
        gr[w, :, y, 0] = gr[w, :, y, 0] + r1[n, 0, 0] + r1[n, 0, 1] + r1[n, 0, 2]
        gr[w, x, :, 1] = gr[w, x, :, 1] + r1[n, 1, 0] + r1[n, 1, 1] + r1[n, 1, 2]
        return [
            send(gr.at[w, (x + d) % 4, y, 0], r2.at[n, 0, d - 1], xp(d))
            for d in (1, 2, 3)
        ] + [
            send(gr.at[w, x, (y + d) % 4, 1], r2.at[n, 1, d - 1], yp(d))
            for d in (1, 2, 3)
        ]

    def scattered(n, w, copies):
        arrive(copies)
        gr[w, x, y] = gr[w, x, y] + r2[n, :, 0] + r2[n, :, 1] + r2[n, :, 2]

    far_s = scatter1(0, far)
    up_s = scatter1(1, up)
    down_s = scatter1(2, down)
    own_s = scatter1(3, zh)

    c1.wait_recv()
    cx[x] = cown[core] + ccore[...]
    c2 = [send(cx.at[x], cx.at[x], xp(d)) for d in (1, 2, 3)]

    h = split(gbm[...] * gcm[...])
    got = dot3(split(ab[...].reshape(128, 256)), h, NN) - pa[...].reshape(128, 256)
    pa[...] = got.reshape(4, 2, 16, 256)
    p1 = send(pa.at[:, other], pcore, twin)

    arrive(c2)
    cy[y] = (cx[0] + cx[1]) + (cx[2] + cx[3])
    c3 = [send(cy.at[y], cy.at[y], yp(d)) for d in (1, 2, 3)]

    p1.wait_recv()
    psum[...] = pa[:, core] + pcore[...]
    p2 = [send(psum.at[(zl + d) % 4], pz.at[d - 1], lp(d)) for d in (1, 2, 3)]

    arrive(c3)
    cz[zl] = (cy[0] + cy[1]) + (cy[2] + cy[3])
    c4 = [send(cz.at[zl], cz.at[zl], lp(d)) for d in (1, 2, 3)]

    far_s = scatter2(0, far, far_s)
    up_s = scatter2(1, up, up_s)
    down_s = scatter2(2, down, down_s)

    arrive(c4)
    ch[0] = (cz[0] + cz[1]) + (cz[2] + cz[3])
    c5 = send(ch.at[0], ch.at[1], at_row(zh + 1 - 2 * (zh % 2), x, y))

    own_s = scatter2(3, zh, own_s)
    scattered(0, far, far_s)
    f_up = send(gr.at[far, x, y, 0], z1.at[0], zp(1))
    f_down = send(gr.at[far, x, y, 1], z1.at[1], zp(3))
    scattered(1, up, up_s)
    scattered(2, down, down_s)

    arrive(p2)
    ga_out[...] = psum[zl] + pz[0] + pz[1] + pz[2]

    c5.wait_recv()
    ch[2] = ch[0] + ch[1]
    c6 = send(ch.at[2], ch.at[3], at_row(3 - zh, x, y))

    f_up.wait_recv()
    gr[up, x, y, 0] = gr[up, x, y, 0] + z1[0]
    l_up = send(gr.at[up, x, y], z2.at[0], zp(1))
    f_down.wait_recv()
    gr[down, x, y, 1] = gr[down, x, y, 1] + z1[1]
    l_down = send(gr.at[down, x, y], z2.at[1], zp(3))
    scattered(3, zh, own_s)

    c6.wait_recv()
    cf[core] = ch[2] + ch[3]
    c7 = send(cf.at[core], cf.at[core], twin)

    arrive([l_up, l_down])
    gbt_out[...] = gr[zh, x, y] + z2[0] + z2[1]
    c7.wait_recv()
    gc_out[:, :128] = cf[0]
    gc_out[:, 128:] = cf[1]
    for copy in sent:
        copy.wait_send()


def local(tensor, factor_a, factor_bt, factor_c):
    bt = factor_bt.reshape(4, 8, 128).transpose(1, 0, 2).reshape(2, 16, 128)
    vmem = pl.BlockSpec(memory_space=pltpu.VMEM)
    grad_a, grad_bt, grad_c = pl.pallas_call(
        kernel,
        out_shape=(
            jax.ShapeDtypeStruct((16, 256), F32),
            jax.ShapeDtypeStruct((2, 16, 128), F32),
            jax.ShapeDtypeStruct((8, 256), F32),
        ),
        in_specs=[pl.BlockSpec(memory_space=pl.ANY), vmem, vmem, vmem],
        out_specs=(vmem, vmem, vmem),
        scratch_shapes=[
            pltpu.VMEM((8, 128, 1024), F32),
            pltpu.VMEM((1024, 1024), BF16),
            pltpu.VMEM((1024, 1024), BF16),
            pltpu.VMEM((256, 1024), BF16),
            pltpu.VMEM((256, 1024), BF16),
            pltpu.VMEM((256, 1024), F32),
            pltpu.VMEM((4, 2, 16, 256), F32),
            pltpu.VMEM((4, 4, 4, 2, 16, 128), F32),
            pltpu.VMEM((8, 256, 128), F32),
            pltpu.VMEM((256, 1024), BF16),
            pltpu.VMEM((256, 1024), BF16),
            pltpu.VMEM((2, 256, 256), BF16),
            pltpu.VMEM((256, 256), F32),
            pltpu.VMEM((256, 256), F32),
            pltpu.VMEM((256, 256), F32),
            pltpu.VMEM((4, 4, 4, 2, 16, 128), F32),
            pltpu.VMEM((4, 2, 3, 4, 16, 128), F32),
            pltpu.VMEM((4, 2, 3, 16, 128), F32),
            pltpu.VMEM((2, 16, 128), F32),
            pltpu.VMEM((2, 2, 16, 128), F32),
            pltpu.VMEM((4, 2, 16, 256), F32),
            pltpu.VMEM((4, 16, 256), F32),
            pltpu.VMEM((4, 16, 256), F32),
            pltpu.VMEM((3, 16, 256), F32),
            pltpu.VMEM((8, 256), F32),
            pltpu.VMEM((2, 8, 128), F32),
            pltpu.VMEM((8, 128), F32),
            pltpu.VMEM((4, 8, 128), F32),
            pltpu.VMEM((4, 8, 128), F32),
            pltpu.VMEM((4, 8, 128), F32),
            pltpu.VMEM((4, 8, 128), F32),
            pltpu.VMEM((2, 8, 128), F32),
            pltpu.VMEM((256, 128), F32),
            pltpu.SemaphoreType.DMA((NSEM,)),
            pltpu.SemaphoreType.DMA((NSEM,)),
            pltpu.SemaphoreType.DMA((3,)),
        ],
        compiler_params=pltpu.CompilerParams(collective_id=0, has_side_effects=True),
    )(tensor, factor_a, bt, factor_c)
    grad_bt = grad_bt.reshape(8, 4, 128).transpose(1, 0, 2).reshape(4, 1024)
    return grad_a, grad_bt, grad_c


def solution(mesh):
    in_specs = (P(None, "row", "col"), P(("row", "col"), None), P("row", "col"), P())
    out_specs = (P(("row", "col"), None), P("row", "col"), P())
    return jax.shard_map(local, mesh=mesh, in_specs=in_specs, out_specs=out_specs, check_vma=False)
```

time: 1440 us -> 71.6 us (0.05)
  waiting for transfers between devices: 1270 us -> 0 us
  blocking collectives: 125 us -> 0 us
  Pallas kernels: 0 us -> 66.5 us
  matrix products: 22.9 us -> 0 us
  between operations: 16.4 us -> 0.64 us
    unnamed x6 -> x0, waiting for transfers between devices: 812 us -> none
    psum x2 -> x0, waiting for transfers between devices: 376 us -> none  [the longest x1 253 us: local(): gram_a = lax.psum(local_gram_a, ('row', 'col'))]
    psum x1 -> x0, blocking collectives: 104 us -> none  [local(): mttkrp_c = lax.psum(partial_c, ('row', 'col'))]
    all_gather x1 -> x0, waiting for transfers between devices: 83.1 us -> none  [local(): block_bt = lax.all_gather(factor_bt, 'row', axis=0, tiled=True)]
    pallas_call x0 -> x1, Pallas kernels: none -> 66.5 us  [local(): pl.pallas_call(kernel, out_shape=(jax.ShapeDtypeStruct((16, 256), F32), j...]
    dot_general x8 -> x0, matrix products: 22.9 us -> none  [the longest x1 6.8 us: local(): jnp.einsum('kir,kij->rj', weighted, tensor, precision=highest)]
    all_gather x1 -> x0, blocking collectives: 20.9 us -> none  [local(): block_a = lax.all_gather(factor_a, 'col', axis=0, tiled=True)]
  transfers between devices with their start and end apart: 5 -> 0, of which waited for: 4 -> 0; matrix products, arithmetic and copies ran while one was open for 2% -> 0% of each run, Pallas kernels for 0% -> 0%
where the time goes in v1:
time: 71.6 us; the launch traced here: 71.1 us
  Pallas kernels  66.5 us (93%)
  local copies, waits for them, and re-layouts  3.94 us (6%)
    pallas_call x1, Pallas kernels, local(): pl.pallas_call(kernel, out_shape=(jax.ShapeDtypeStruct((16, 256), F32), j...  66.5 us
    unnamed x3, local copies, waits for them, and re-layouts  3.94 us

profile of v1, /device:TPU:1, one launch (start us, length us, event | category | flops | bytes accessed | tf_op | source)
XLA Modules:
  0.0 71.1 jit_solution(7838583895516817759)
XLA Ops:
  0.6 66.5 %shard_map.67 = (f32[16,256]{1,0:T(8,128)}, f32[2,16,128]{2,1,0:T(8,128)}, f32[8,256]{1,0:T(8,128)}) custom-call(f32[8,128,1024]{2,1,0:T(8,128)} %t_hbm.1, f32[16,256]{1,0:T(8,128)} %a_ref.1, f32[2,16,128]{2,1,0:T(8,128)} %bitcast.10, f32[8,256]{1,0:T(8,128)} %c_ref.1), custom_call_target="tpu_custom_call" | custom-call | tf_op jit(solution)/shard_map/pallas_call | solution.py:299
  67.2 1.3 %copy.12 = f32[16,256]{1,0:T(8,128)} copy(f32[16,256]{1,0:T(8,128)} %get-tuple-element.12) | data formatting | bytes 32768
  68.5 1.3 %copy.13 = f32[4,1024]{1,0:T(4,128)} copy(f32[4,1024]{1,0:T(4,128)} %bitcast.11) | data formatting | bytes 32768
  69.8 1.3 %copy.14 = f32[8,256]{1,0:T(8,128)} copy(f32[8,256]{1,0:T(8,128)} %get-tuple-element.14) | data formatting | bytes 16384

commit v2 on v0

v2 whole, which is shorter than its diff:
```python
import jax
import jax.numpy as jnp
from jax import lax
from jax.experimental import pallas as pl
from jax.experimental.pallas import tpu as pltpu
from jax.sharding import PartitionSpec as P

MESH = pl.DeviceIdType.MESH
F32, BF16 = jnp.float32, jnp.bfloat16
NSEM = 176
NN = (((1,), (0,)), ((), ()))
NT = (((1,), (1,)), ((), ()))
PLANE = [(i, j) for i in range(4) for j in range(4) if i or j]


def split(v):
    hi = v.astype(BF16)
    return hi, (v - hi.astype(F32)).astype(BF16)


def dot3(a, b, dims):
    def one(u, v):
        return lax.dot_general(u, v, dims, preferred_element_type=F32)

    return one(a[0], b[0]) + (one(a[0], b[1]) + one(a[1], b[0]))


def added(parts):
    while len(parts) > 1:
        parts = [a + b for a, b in zip(parts[::2], parts[1::2])] + parts[len(parts) & ~1 :]
    return parts[0]


def kernel(
    t_hbm, a_hbm, bt_hbm, c_hbm,
    ga_hbm, gbt_hbm, gc_hbm,
    tf, thi, tlo, whi, wlo, m1, ab, bg, btn, bhi, blo, hm, gam, gcm, gbm,
    gr, r1, z1, z2, pa, pcore, psum, pz, pck, cp, cz, ch,
    cv, at, ct, ga_out, gbt_out, gc_out, ssem, rsem, lsem,
):
    row, col = lax.axis_index("row"), lax.axis_index("col")
    zh, x, y = row // 16, (row // 4) % 4, row % 4
    zl, core = col // 2, col % 2
    other = 1 - core
    here = x * 4 + y
    up, down, far = (zh + 1) % 4, (zh + 3) % 4, (zh + 2) % 4

    def pp(d):
        return (zh * 16 + ((x + d[0]) % 4) * 4 + (y + d[1]) % 4, col)

    def zp(d):
        return (((zh + d) % 4) * 16 + here, col)

    def lp(d, c):
        return (row, ((zl + d) % 4) * 2 + c)

    twin = (row, zl * 2 + other)
    column = [lp(d, c) for d in (1, 2, 3) for c in (core, other)] + [twin]
    sent = []

    def send(src, dst, device):
        k = len(sent)
        copy = pltpu.make_async_remote_copy(
            src_ref=src, dst_ref=dst, send_sem=ssem.at[k], recv_sem=rsem.at[k],
            device_id=device, device_id_type=MESH,
        )
        copy.start()
        sent.append(copy)
        return copy

    def arrive(copies):
        for copy in copies:
            copy.wait_recv()

    barrier = pltpu.get_barrier_semaphore()
    peers = [zp(1), zp(3)] + [pp(d) for d in PLANE] + column
    for device in peers:
        pl.semaphore_signal(barrier, inc=1, device_id=device, device_id_type=MESH)
    loads = [
        pltpu.make_async_copy(src, dst, lsem.at[k])
        for k, (src, dst) in enumerate(
            [(bt_hbm, bg.at[zh, x, y]), (a_hbm, ab.at[zl, core]), (c_hbm, cv), (t_hbm, tf)]
        )
    ]
    for load in loads:
        load.start()
    for load in loads[:3]:
        load.wait()
    pl.semaphore_wait(barrier, len(peers))

    def spread(w):
        mine = bg.at[w, x, y]
        return [send(mine, mine, pp(d)) for d in PLANE]

    mine = bg.at[zh, x, y]
    z_up = send(mine, mine, zp(1))
    z_down = send(mine, mine, zp(3))
    own_w = spread(zh)

    loads[3].wait()

    def split_t(k, _):
        hi, lo = split(tf[k])
        rows = pl.ds(pl.multiple_of(k * 128, 128), 128)
        thi[rows, :] = hi
        tlo[rows, :] = lo
        return 0

    lax.fori_loop(0, 8, split_t, 0)
    a_line = [send(ab.at[zl, core], ab.at[zl, core], lp(d, core)) for d in (1, 2, 3)]

    ct[...] = jnp.transpose(jnp.concatenate([cv[...], jnp.zeros((120, 256), F32)], 0))
    c_t = split(ct[...])
    gcm[...] = dot3(c_t, c_t, NT)

    def permuted(ref):
        return jnp.concatenate([ref[pl.ds(q, 64, stride=4), :] for q in range(4)], 0)

    ct_p = permuted(ct)

    z_up.wait_recv()
    half = bg.at[down, x, y, 0]
    on_up = send(half, half, zp(1))
    z_down.wait_recv()
    half = bg.at[up, x, y, 1]
    on_down = send(half, half, zp(3))
    down_w = spread(down)
    up_w = spread(up)

    arrive(a_line)
    a_twin = send(ab.at[:, core], ab.at[:, core], twin)

    bg2 = bg.reshape(2048, 128)

    def ordered(w, copies):
        arrive(copies)
        rows = pl.ds(pl.multiple_of(w * 64, 64), 64)
        for j in range(8):
            for q in range(4):
                btn[j, pl.ds(w * 64 + q, 16, stride=4), :] = bg2[
                    pl.ds(w * 512 + j * 4 + q, 16, stride=32), :
                ]
        for j in range(8):
            hi, lo = split(btn[j, rows, :])
            bhi[rows, j * 128 : (j + 1) * 128] = hi
            blo[rows, j * 128 : (j + 1) * 128] = lo

    ordered(zh, own_w)

    a_twin.wait_recv()
    at[...] = jnp.transpose(ab[...].reshape(128, 256))
    a_t = split(at[...])
    gam[...] = dot3(a_t, a_t, NT)
    at_p = permuted(at)
    h = dot3(split(at_p), a_t, NT) * dot3(split(ct_p), c_t, NT)
    hm[0], hm[1] = split(h)

    arrive([on_up, on_down])
    far_w = spread(far)

    for k in range(8):
        hi, lo = split(at_p * ct_p[:, k : k + 1])
        whi[:, k * 128 : (k + 1) * 128] = hi
        wlo[:, k * 128 : (k + 1) * 128] = lo

    def first(j, _):
        cols = pl.ds(pl.multiple_of(j * 256, 256), 256)
        m1[:, cols] = dot3((whi[...], wlo[...]), (thi[:, cols], tlo[:, cols]), NN)
        return 0

    lax.fori_loop(0, 4, first, 0)
    ordered(down, down_w)
    ordered(up, up_w)
    pa[...] = jnp.zeros_like(pa)
    arrive(far_w)
    ordered(far, [])

    b_split = (bhi[...], blo[...])
    gbm[...] = dot3(b_split, b_split, NT)

    def second(m, _):
        rows = pl.ds(pl.multiple_of(m * 512, 512), 512)
        part = dot3((thi[rows, :], tlo[rows, :]), (bhi[...], blo[...]), NT)
        rows_a = ab[...].reshape(128, 256)
        acc = pa[...].reshape(128, 256)
        for k in range(4):
            one = part[k * 128 : (k + 1) * 128]
            acc = acc + one * cv[pl.ds(m * 4 + k, 1), :]
            pck[pl.ds(m * 4 + k, 1), :] = jnp.sum(one * rows_a, axis=0, keepdims=True)
        pa[...] = acc.reshape(4, 2, 16, 256)
        return 0

    lax.fori_loop(0, 2, second, 0)
    cp[here] = dot3(split(cv[...]), split(gam[...] * gbm[...]), NN) - pck[...]
    c1 = [send(cp.at[here], cp.at[here], pp(d)) for d in PLANE]

    gr2 = gr.reshape(2048, 128)
    for j in range(4):
        cols = slice(j * 256, (j + 1) * 256)
        got = dot3((hm[0], hm[1]), (bhi[:, cols], blo[:, cols]), NN) - m1[:, cols]
        for i in range(2):
            for q in range(4):
                gr2[pl.ds((j * 2 + i) * 4 + q, 64, stride=32), :] = got[
                    q * 64 : (q + 1) * 64, i * 128 : (i + 1) * 128
                ]

    def scatter(n, w):
        return [
            send(gr.at[w, (x + d[0]) % 4, (y + d[1]) % 4], r1.at[n, i], pp(d))
            for i, d in enumerate(PLANE)
        ]

    def gathered(n, w, copies):
        arrive(copies)
        gr[w, x, y] = gr[w, x, y] + added([r1[n, i] for i in range(15)])

    far_s = scatter(0, far)
    up_s = scatter(1, up)
    down_s = scatter(2, down)

    h = split(gbm[...] * gcm[...])
    got = dot3(split(ab[...].reshape(128, 256)), h, NN) - pa[...].reshape(128, 256)
    pa[...] = got.reshape(4, 2, 16, 256)
    p1 = send(pa.at[:, other], pcore, twin)

    arrive(c1)
    cz[col] = added([cp[i] for i in range(16)])
    c2 = [send(cz.at[col], cz.at[col], device) for device in column]
    own_s = scatter(3, zh)

    p1.wait_recv()
    psum[...] = pa[:, core] + pcore[...]
    p2 = [send(psum.at[(zl + d) % 4], pz.at[d - 1], lp(d, core)) for d in (1, 2, 3)]

    gathered(0, far, far_s)
    f_up = send(gr.at[far, x, y, 0], z1.at[0], zp(1))
    f_down = send(gr.at[far, x, y, 1], z1.at[1], zp(3))

    arrive(c2)
    ch[zh] = added([cz[i] for i in range(8)])
    c3 = [send(ch.at[zh], ch.at[zh], zp(d)) for d in (2, 1, 3)]

    gathered(1, up, up_s)
    gathered(2, down, down_s)
    f_up.wait_recv()
    gr[up, x, y, 0] = gr[up, x, y, 0] + z1[0]
    l_up = send(gr.at[up, x, y], z2.at[0], zp(1))
    f_down.wait_recv()
    gr[down, x, y, 1] = gr[down, x, y, 1] + z1[1]
    l_down = send(gr.at[down, x, y], z2.at[1], zp(3))

    arrive(p2)
    ga_out[...] = psum[zl] + pz[0] + pz[1] + pz[2]
    stores = [pltpu.make_async_copy(ga_out, ga_hbm, lsem.at[0])]
    stores[0].start()
    gathered(3, zh, own_s)

    arrive([l_up, l_down])
    gbt_out[...] = gr[zh, x, y] + z2[0] + z2[1]
    stores.append(pltpu.make_async_copy(gbt_out, gbt_hbm, lsem.at[1]))
    stores[1].start()
    arrive(c3)
    gc_out[...] = added([ch[i] for i in range(4)])
    stores.append(pltpu.make_async_copy(gc_out, gc_hbm, lsem.at[2]))
    stores[2].start()
    for copy in sent:
        copy.wait_send()
    for store in stores:
        store.wait()


def last(a_in, b_in, c_in, a_out, b_out, c_out):
    a_out[...] = a_in[...]
    b_out[...] = b_in[...]
    c_out[...] = c_in[...]


def local(tensor, factor_a, factor_bt, factor_c):
    bt = factor_bt.reshape(4, 8, 128).transpose(1, 0, 2).reshape(2, 16, 128)
    shapes = (
        jax.ShapeDtypeStruct((16, 256), F32),
        jax.ShapeDtypeStruct((2, 16, 128), F32),
        jax.ShapeDtypeStruct((8, 256), F32),
    )
    anywhere, vmem = pl.BlockSpec(memory_space=pl.ANY), pl.BlockSpec(memory_space=pltpu.VMEM)
    parts = pl.pallas_call(
        kernel,
        out_shape=shapes,
        in_specs=[anywhere] * 4,
        out_specs=(anywhere,) * 3,
        scratch_shapes=[
            pltpu.VMEM((8, 128, 1024), F32),
            pltpu.VMEM((1024, 1024), BF16),
            pltpu.VMEM((1024, 1024), BF16),
            pltpu.VMEM((256, 1024), BF16),
            pltpu.VMEM((256, 1024), BF16),
            pltpu.VMEM((256, 1024), F32),
            pltpu.VMEM((4, 2, 16, 256), F32),
            pltpu.VMEM((4, 4, 4, 2, 16, 128), F32),
            pltpu.VMEM((8, 256, 128), F32),
            pltpu.VMEM((256, 1024), BF16),
            pltpu.VMEM((256, 1024), BF16),
            pltpu.VMEM((2, 256, 256), BF16),
            pltpu.VMEM((256, 256), F32),
            pltpu.VMEM((256, 256), F32),
            pltpu.VMEM((256, 256), F32),
            pltpu.VMEM((4, 4, 4, 2, 16, 128), F32),
            pltpu.VMEM((4, 15, 2, 16, 128), F32),
            pltpu.VMEM((2, 16, 128), F32),
            pltpu.VMEM((2, 2, 16, 128), F32),
            pltpu.VMEM((4, 2, 16, 256), F32),
            pltpu.VMEM((4, 16, 256), F32),
            pltpu.VMEM((4, 16, 256), F32),
            pltpu.VMEM((3, 16, 256), F32),
            pltpu.VMEM((8, 256), F32),
            pltpu.VMEM((16, 8, 256), F32),
            pltpu.VMEM((8, 8, 256), F32),
            pltpu.VMEM((4, 8, 256), F32),
            pltpu.VMEM((8, 256), F32),
            pltpu.VMEM((256, 128), F32),
            pltpu.VMEM((256, 128), F32),
            pltpu.VMEM((16, 256), F32),
            pltpu.VMEM((2, 16, 128), F32),
            pltpu.VMEM((8, 256), F32),
            pltpu.SemaphoreType.DMA((NSEM,)),
            pltpu.SemaphoreType.DMA((NSEM,)),
            pltpu.SemaphoreType.DMA((4,)),
        ],
        compiler_params=pltpu.CompilerParams(collective_id=0, has_side_effects=True),
    )(tensor, factor_a, bt, factor_c)
    grad_a, grad_bt, grad_c = pl.pallas_call(
        last, out_shape=shapes, in_specs=[vmem] * 3, out_specs=(vmem,) * 3
    )(*parts)
    grad_bt = grad_bt.reshape(8, 4, 128).transpose(1, 0, 2).reshape(4, 1024)
    return grad_a, grad_bt, grad_c


def solution(mesh):
    in_specs = (P(None, "row", "col"), P(("row", "col"), None), P("row", "col"), P())
    out_specs = (P(("row", "col"), None), P("row", "col"), P())
    return jax.shard_map(local, mesh=mesh, in_specs=in_specs, out_specs=out_specs, check_vma=False)
```

time: 1440 us -> 57.6 us (0.04)
  the two profiles are of different devices: /device:TPU:1 before, /device:TPU:32 now
where the time goes in v2:
time: 57.6 us; the launch traced here: 57.3 us
  Pallas kernels  56.7 us (98%)
  between operations  0.64 us (1%)
    pallas_call x1, Pallas kernels, local(): pl.pallas_call(kernel, out_shape=shapes, in_specs=[anywhere] * 4, out_spe...  55.3 us
    pallas_call x1, Pallas kernels, local(): pl.pallas_call(last, out_shape=shapes, in_specs=[vmem] * 3, out_specs=(vm...  1.35 us

profile of v2, /device:TPU:32, one launch (start us, length us, event | category | flops | bytes accessed | tf_op | source)
XLA Modules:
  0.0 57.3 jit_solution(10555066974589636030)
XLA Ops:
  0.6 55.3 %shard_map.67 = (f32[16,256]{1,0:T(8,128)}, f32[2,16,128]{2,1,0:T(8,128)}, f32[8,256]{1,0:T(8,128)}) custom-call(f32[8,128,1024]{2,1,0:T(8,128)} %t_hbm.1, f32[16,256]{1,0:T(8,128)} %a_hbm.1, f32[2,16,128]{2,1,0:T(8,128)} %bitcast.10, f32[8,256]{1,0:T(8,128)} %c_hbm.1), custom_call_target="tpu_custom_call" | custom-call | tf_op jit(solution)/shard_map/pallas_call | solution.py:286
  56.0 1.4 %shard_map.68 = (f32[16,256]{1,0:T(8,128)}, f32[2,16,128]{2,1,0:T(8,128)}, f32[8,256]{1,0:T(8,128)}) custom-call(f32[16,256]{1,0:T(8,128)} %get-tuple-element.9.a_in, f32[2,16,128]{2,1,0:T(8,128)} %get-tuple-element.10.b_in, f32[8,256]{1,0:T(8,128)} %get-tuple-element.11.c_in), custom_call_target="tpu_custom_call" | custom-call | tf_op jit(solution)/shard_map/pallas_call | solution.py:331

commit v3 on v2

--- a/solution.py
+++ b/solution.py
@@ -10,7 +10,10 @@
 NSEM = 176
 NN = (((1,), (0,)), ((), ()))
 NT = (((1,), (1,)), ((), ()))
-PLANE = [(i, j) for i in range(4) for j in range(4) if i or j]
+PLANE = sorted(
+    ((i, j) for i in range(4) for j in range(4) if i or j),
+    key=lambda d: -min(d[0], 4 - d[0]) - min(d[1], 4 - d[1]),
+)
 
 
 def split(v):
@@ -33,9 +36,9 @@
 
 def kernel(
     t_hbm, a_hbm, bt_hbm, c_hbm,
-    ga_hbm, gbt_hbm, gc_hbm,
-    tf, thi, tlo, whi, wlo, m1, ab, bg, btn, bhi, blo, hm, gam, gcm, gbm,
-    gr, r1, z1, z2, pa, pcore, psum, pz, pck, cp, cz, ch,
+    ga_res, gbt_res, gc_res,
+    tf, thi, tlo, whi, wlo, ab, bg, btn, bhi, blo, gam, gcm, gbm,
+    gr, r1a, r1b, r2a, r2b, z1a, z1b, z2, pa, pcore, psum, pz, pck, cp, cz, ch,
     cv, at, ct, ga_out, gbt_out, gc_out, ssem, rsem, lsem,
 ):
     row, col = lax.axis_index("row"), lax.axis_index("col")
@@ -84,18 +87,16 @@
     ]
     for load in loads:
         load.start()
-    for load in loads[:3]:
-        load.wait()
     pl.semaphore_wait(barrier, len(peers))
 
-    def spread(w):
-        mine = bg.at[w, x, y]
-        return [send(mine, mine, pp(d)) for d in PLANE]
-
-    mine = bg.at[zh, x, y]
-    z_up = send(mine, mine, zp(1))
-    z_down = send(mine, mine, zp(3))
-    own_w = spread(zh)
+    def spread(w, src):
+        return [send(src, bg.at[w, x, y], pp(d)) for d in PLANE]
+
+    z_up = [send(bt_hbm.at[0], bg.at[zh, x, y, 0], zp(1))]
+    z_down = [send(bt_hbm.at[1], bg.at[zh, x, y, 1], zp(3))]
+    z_up.append(send(bt_hbm.at[1], bg.at[zh, x, y, 1], zp(1)))
+    z_down.append(send(bt_hbm.at[0], bg.at[zh, x, y, 0], zp(3)))
+    own_w = spread(zh, bt_hbm)
 
     loads[3].wait()
 
@@ -107,8 +108,9 @@
         return 0
 
     lax.fori_loop(0, 8, split_t, 0)
-    a_line = [send(ab.at[zl, core], ab.at[zl, core], lp(d, core)) for d in (1, 2, 3)]
-
+
+    for load in loads[:3]:
+        load.wait()
     ct[...] = jnp.transpose(jnp.concatenate([cv[...], jnp.zeros((120, 256), F32)], 0))
     c_t = split(ct[...])
     gcm[...] = dot3(c_t, c_t, NT)
@@ -118,14 +120,17 @@
 
     ct_p = permuted(ct)
 
-    z_up.wait_recv()
+    a_line = [send(a_hbm, ab.at[zl, core], lp(d, core)) for d in (1, 2, 3)]
+    z_up[0].wait_recv()
     half = bg.at[down, x, y, 0]
     on_up = send(half, half, zp(1))
-    z_down.wait_recv()
+    z_down[0].wait_recv()
     half = bg.at[up, x, y, 1]
     on_down = send(half, half, zp(3))
-    down_w = spread(down)
-    up_w = spread(up)
+    z_up[1].wait_recv()
+    down_w = spread(down, bg.at[down, x, y])
+    z_down[1].wait_recv()
+    up_w = spread(up, bg.at[up, x, y])
 
     arrive(a_line)
     a_twin = send(ab.at[:, core], ab.at[:, core], twin)
@@ -152,28 +157,66 @@
     a_t = split(at[...])
     gam[...] = dot3(a_t, a_t, NT)
     at_p = permuted(at)
-    h = dot3(split(at_p), a_t, NT) * dot3(split(ct_p), c_t, NT)
-    hm[0], hm[1] = split(h)
+    gr2 = gr.reshape(2560, 128)
+    part = dot3(split(at_p), a_t, NT)
+    for i in range(2):
+        for q in range(4):
+            gr2[pl.ds(32 + i * 4 + q, 64, stride=40), :] = part[
+                q * 64 : (q + 1) * 64, i * 128 : (i + 1) * 128
+            ]
 
     arrive([on_up, on_down])
-    far_w = spread(far)
+    far_w = spread(far, bg.at[far, x, y])
 
     for k in range(8):
         hi, lo = split(at_p * ct_p[:, k : k + 1])
         whi[:, k * 128 : (k + 1) * 128] = hi
         wlo[:, k * 128 : (k + 1) * 128] = lo
 
-    def first(j, _):
-        cols = pl.ds(pl.multiple_of(j * 256, 256), 256)
-        m1[:, cols] = dot3((whi[...], wlo[...]), (thi[:, cols], tlo[:, cols]), NN)
-        return 0
-
-    lax.fori_loop(0, 4, first, 0)
+    for j in range(4):
+        cols = slice(j * 256, (j + 1) * 256)
+        got = dot3((whi[...], wlo[...]), (thi[:, cols], tlo[:, cols]), NN)
+        for i in range(2):
+            for q in range(4):
+                gr2[pl.ds((j * 2 + i) * 4 + q, 64, stride=40), :] = got[
+                    q * 64 : (q + 1) * 64, i * 128 : (i + 1) * 128
+                ]
+
+    one, two = pl.ds(0, 2), pl.ds(2, 3)
+
+    def scatter1(n, w):
+        return [
+            send(gr.at[w, :, (y + d) % 4, one], r1a.at[n, d - 1], pp((0, d)))
+            for d in (2, 1, 3)
+        ] + [
+            send(gr.at[w, (x + d) % 4, :, two], r1b.at[n, d - 1], pp((d, 0)))
+            for d in (2, 1, 3)
+        ]
+
+    def scatter2(n, w, copies):
+        arrive(copies)
+        gr[w, :, y, one] = gr[w, :, y, one] + added([r1a[n, i] for i in range(3)])
+        gr[w, x, :, two] = gr[w, x, :, two] + added([r1b[n, i] for i in range(3)])
+        return [
+            send(gr.at[w, (x + d) % 4, y, one], r2a.at[n, d - 1], pp((d, 0)))
+            for d in (2, 1, 3)
+        ] + [
+            send(gr.at[w, x, (y + d) % 4, two], r2b.at[n, d - 1], pp((0, d)))
+            for d in (2, 1, 3)
+        ]
+
+    def gathered(n, w, copies):
+        arrive(copies)
+        gr[w, x, y, one] = gr[w, x, y, one] + added([r2a[n, i] for i in range(3)])
+        gr[w, x, y, two] = gr[w, x, y, two] + added([r2b[n, i] for i in range(3)])
+
     ordered(down, down_w)
     ordered(up, up_w)
     pa[...] = jnp.zeros_like(pa)
     arrive(far_w)
+    far_s = scatter1(0, far)
     ordered(far, [])
+    up_s = scatter1(1, up)
 
     b_split = (bhi[...], blo[...])
     gbm[...] = dot3(b_split, b_split, NT)
@@ -194,74 +237,64 @@
     cp[here] = dot3(split(cv[...]), split(gam[...] * gbm[...]), NN) - pck[...]
     c1 = [send(cp.at[here], cp.at[here], pp(d)) for d in PLANE]
 
-    gr2 = gr.reshape(2048, 128)
-    for j in range(4):
-        cols = slice(j * 256, (j + 1) * 256)
-        got = dot3((hm[0], hm[1]), (bhi[:, cols], blo[:, cols]), NN) - m1[:, cols]
-        for i in range(2):
-            for q in range(4):
-                gr2[pl.ds((j * 2 + i) * 4 + q, 64, stride=32), :] = got[
-                    q * 64 : (q + 1) * 64, i * 128 : (i + 1) * 128
-                ]
-
-    def scatter(n, w):
-        return [
-            send(gr.at[w, (x + d[0]) % 4, (y + d[1]) % 4], r1.at[n, i], pp(d))
-            for i, d in enumerate(PLANE)
-        ]
-
-    def gathered(n, w, copies):
-        arrive(copies)
-        gr[w, x, y] = gr[w, x, y] + added([r1[n, i] for i in range(15)])
-
-    far_s = scatter(0, far)
-    up_s = scatter(1, up)
-    down_s = scatter(2, down)
+    down_s = scatter1(2, down)
 
     h = split(gbm[...] * gcm[...])
     got = dot3(split(ab[...].reshape(128, 256)), h, NN) - pa[...].reshape(128, 256)
     pa[...] = got.reshape(4, 2, 16, 256)
     p1 = send(pa.at[:, other], pcore, twin)
 
+    far_s = scatter2(0, far, far_s)
+    up_s = scatter2(1, up, up_s)
+
     arrive(c1)
     cz[col] = added([cp[i] for i in range(16)])
     c2 = [send(cz.at[col], cz.at[col], device) for device in column]
-    own_s = scatter(3, zh)
+    down_s = scatter2(2, down, down_s)
+    gathered(0, far, far_s)
+    f_up = send(gr.at[far, x, y, one], z1a, zp(1))
+    f_down = send(gr.at[far, x, y, two], z1b, zp(3))
+    own_s = scatter1(3, zh)
 
     p1.wait_recv()
     psum[...] = pa[:, core] + pcore[...]
     p2 = [send(psum.at[(zl + d) % 4], pz.at[d - 1], lp(d, core)) for d in (1, 2, 3)]
-
-    gathered(0, far, far_s)
-    f_up = send(gr.at[far, x, y, 0], z1.at[0], zp(1))
-    f_down = send(gr.at[far, x, y, 1], z1.at[1], zp(3))
+    gathered(1, up, up_s)
+    gathered(2, down, down_s)
 
     arrive(c2)
     ch[zh] = added([cz[i] for i in range(8)])
     c3 = [send(ch.at[zh], ch.at[zh], zp(d)) for d in (2, 1, 3)]
 
-    gathered(1, up, up_s)
-    gathered(2, down, down_s)
     f_up.wait_recv()
-    gr[up, x, y, 0] = gr[up, x, y, 0] + z1[0]
+    gr[up, x, y, one] = gr[up, x, y, one] + z1a[...]
     l_up = send(gr.at[up, x, y], z2.at[0], zp(1))
     f_down.wait_recv()
-    gr[down, x, y, 1] = gr[down, x, y, 1] + z1[1]
+    gr[down, x, y, two] = gr[down, x, y, two] + z1b[...]
     l_down = send(gr.at[down, x, y], z2.at[1], zp(3))
+    own_s = scatter2(3, zh, own_s)
 
     arrive(p2)
     ga_out[...] = psum[zl] + pz[0] + pz[1] + pz[2]
-    stores = [pltpu.make_async_copy(ga_out, ga_hbm, lsem.at[0])]
+    stores = [
+        pltpu.make_async_copy(src, dst, lsem.at[k])
+        for k, (src, dst) in enumerate([(ga_out, ga_res), (gbt_out, gbt_res), (gc_out, gc_res)])
+    ]
     stores[0].start()
     gathered(3, zh, own_s)
 
     arrive([l_up, l_down])
-    gbt_out[...] = gr[zh, x, y] + z2[0] + z2[1]
-    stores.append(pltpu.make_async_copy(gbt_out, gbt_hbm, lsem.at[1]))
+    got = gr[zh, x, y] + z2[0] + z2[1]
+    gram_a = jnp.concatenate([got[4, :4], got[4, 4:]], 1)
+    gram_c = jnp.concatenate([gcm[pl.ds(row * 4 + q, 1), :] for q in range(4)], 0)
+    h = jnp.concatenate([gram_a * gram_c, jnp.zeros((12, 256), F32)], 0)
+    h = dot3(split(h), (bhi[...], blo[...]), NN)[:4]
+    for t in range(4):
+        two = [h[:, (2 * t + i) * 128 : (2 * t + i + 1) * 128] for i in range(2)]
+        gbt_out[t] = jnp.concatenate(two, 0) - got[t]
     stores[1].start()
     arrive(c3)
     gc_out[...] = added([ch[i] for i in range(4)])
-    stores.append(pltpu.make_async_copy(gc_out, gc_hbm, lsem.at[2]))
     stores[2].start()
     for copy in sent:
         copy.wait_send()
@@ -279,35 +312,37 @@
     bt = factor_bt.reshape(4, 8, 128).transpose(1, 0, 2).reshape(2, 16, 128)
     shapes = (
         jax.ShapeDtypeStruct((16, 256), F32),
-        jax.ShapeDtypeStruct((2, 16, 128), F32),
+        jax.ShapeDtypeStruct((4, 8, 128), F32),
         jax.ShapeDtypeStruct((8, 256), F32),
     )
-    anywhere, vmem = pl.BlockSpec(memory_space=pl.ANY), pl.BlockSpec(memory_space=pltpu.VMEM)
+    vmem = pl.BlockSpec(memory_space=pltpu.VMEM)
     parts = pl.pallas_call(
         kernel,
-        out_shape=shapes,
-        in_specs=[anywhere] * 4,
-        out_specs=(anywhere,) * 3,
+        out_shape=tuple(pltpu.VMEM(v.shape, v.dtype) for v in shapes),
+        in_specs=[pl.BlockSpec(memory_space=pltpu.HBM)] * 4,
+        out_specs=(pl.BlockSpec(memory_space=pl.ANY),) * 3,
         scratch_shapes=[
             pltpu.VMEM((8, 128, 1024), F32),
             pltpu.VMEM((1024, 1024), BF16),
             pltpu.VMEM((1024, 1024), BF16),
             pltpu.VMEM((256, 1024), BF16),
             pltpu.VMEM((256, 1024), BF16),
-            pltpu.VMEM((256, 1024), F32),
             pltpu.VMEM((4, 2, 16, 256), F32),
             pltpu.VMEM((4, 4, 4, 2, 16, 128), F32),
             pltpu.VMEM((8, 256, 128), F32),
             pltpu.VMEM((256, 1024), BF16),
             pltpu.VMEM((256, 1024), BF16),
-            pltpu.VMEM((2, 256, 256), BF16),
             pltpu.VMEM((256, 256), F32),
             pltpu.VMEM((256, 256), F32),
             pltpu.VMEM((256, 256), F32),
-            pltpu.VMEM((4, 4, 4, 2, 16, 128), F32),
-            pltpu.VMEM((4, 15, 2, 16, 128), F32),
-            pltpu.VMEM((2, 16, 128), F32),
-            pltpu.VMEM((2, 2, 16, 128), F32),
+            pltpu.VMEM((4, 4, 4, 5, 8, 128), F32),
+            pltpu.VMEM((4, 3, 4, 2, 8, 128), F32),
+            pltpu.VMEM((4, 3, 4, 3, 8, 128), F32),
+            pltpu.VMEM((4, 3, 2, 8, 128), F32),
+            pltpu.VMEM((4, 3, 3, 8, 128), F32),
+            pltpu.VMEM((2, 8, 128), F32),
+            pltpu.VMEM((3, 8, 128), F32),
+            pltpu.VMEM((2, 5, 8, 128), F32),
             pltpu.VMEM((4, 2, 16, 256), F32),
             pltpu.VMEM((4, 16, 256), F32),
             pltpu.VMEM((4, 16, 256), F32),
@@ -320,7 +355,7 @@
             pltpu.VMEM((256, 128), F32),
             pltpu.VMEM((256, 128), F32),
             pltpu.VMEM((16, 256), F32),
-            pltpu.VMEM((2, 16, 128), F32),
+            pltpu.VMEM((4, 8, 128), F32),
             pltpu.VMEM((8, 256), F32),
             pltpu.SemaphoreType.DMA((NSEM,)),
             pltpu.SemaphoreType.DMA((NSEM,)),
@@ -330,7 +365,7 @@
     )(tensor, factor_a, bt, factor_c)
     grad_a, grad_bt, grad_c = pl.pallas_call(
         last, out_shape=shapes, in_specs=[vmem] * 3, out_specs=(vmem,) * 3
-    )(*parts)
+    )(*(pltpu.with_memory_space_constraint(v, pltpu.VMEM) for v in parts))
     grad_bt = grad_bt.reshape(8, 4, 128).transpose(1, 0, 2).reshape(4, 1024)
     return grad_a, grad_bt, grad_c
 

time: 57.6 us -> 53.9 us (0.936)
  the two profiles are of different devices: /device:TPU:32 before, /device:TPU:1 now
where the time goes in v3:
time: 53.9 us; the launch traced here: 53.8 us
  Pallas kernels  53.2 us (99%)
  between operations  0.64 us (1%)
    pallas_call x1, Pallas kernels, local(): pl.pallas_call(kernel, out_shape=tuple((pltpu.VMEM(v.shape, v.dtype) for...  52.5 us

profile of v3, /device:TPU:1, one launch (start us, length us, event | category | flops | bytes accessed | tf_op | source)
XLA Modules:
  0.0 53.8 jit_solution(332175693345069021)
XLA Ops:
  0.6 52.5 %shard_map.67 = (f32[16,256]{1,0:T(8,128)S(1)}, f32[4,8,128]{2,1,0:T(8,128)S(1)}, f32[8,256]{1,0:T(8,128)S(1)}) custom-call(f32[8,128,1024]{2,1,0:T(8,128)} %t_hbm.1, f32[16,256]{1,0:T(8,128)} %a_hbm.1, f32[2,16,128]{2,1,0:T(8,128)} %bitcast.10, f32[8,256]{1,0:T(8,128)} %c_hbm.1), custom_call_target="tpu_custom_call" | custom-call | tf_op jit(solution)/shard_map/pallas_call | solution.py:319
  53.2 0.6 %shard_map.68 = (f32[16,256]{1,0:T(8,128)}, f32[4,8,128]{2,1,0:T(8,128)}, f32[8,256]{1,0:T(8,128)}) custom-call(f32[16,256]{1,0:T(8,128)S(1)} %get-tuple-element.9.a_in, f32[4,8,128]{2,1,0:T(8,128)S(1)} %get-tuple-element.10.b_in, f32[8,256]{1,0:T(8,128)S(1)} %get-tuple-element.11.c_in), custom_call_target="tpu_custom_call" | custom-call | tf_op jit(solution)/shard_map/pallas_call | solution.py:366

commit v4 on v3

--- a/solution.py
+++ b/solution.py
@@ -7,7 +7,7 @@
 
 MESH = pl.DeviceIdType.MESH
 F32, BF16 = jnp.float32, jnp.bfloat16
-NSEM = 176
+NSEM = 32
 NN = (((1,), (0,)), ((), ()))
 NT = (((1,), (1,)), ((), ()))
 PLANE = sorted(
@@ -37,7 +37,7 @@
 def kernel(
     t_hbm, a_hbm, bt_hbm, c_hbm,
     ga_res, gbt_res, gc_res,
-    tf, thi, tlo, whi, wlo, ab, bg, btn, bhi, blo, gam, gcm, gbm,
+    tf, thi, tlo, whi, wlo, ab, bg, btn, gam, gcm, gbm,
     gr, r1a, r1b, r2a, r2b, z1a, z1b, z2, pa, pcore, psum, pz, pck, cp, cz, ch,
     cv, at, ct, ga_out, gbt_out, gc_out, ssem, rsem, lsem,
 ):
@@ -59,21 +59,22 @@
 
     twin = (row, zl * 2 + other)
     column = [lp(d, c) for d in (1, 2, 3) for c in (core, other)] + [twin]
-    sent = []
-
-    def send(src, dst, device):
-        k = len(sent)
-        copy = pltpu.make_async_remote_copy(
-            src_ref=src, dst_ref=dst, send_sem=ssem.at[k], recv_sem=rsem.at[k],
-            device_id=device, device_id_type=MESH,
-        )
-        copy.start()
-        sent.append(copy)
-        return copy
-
-    def arrive(copies):
-        for copy in copies:
-            copy.wait_recv()
+    groups = []
+    slots = bg.reshape(64, 2, 16, 128).at[pl.ds(0, 15)]
+
+    def send(copies, sized):
+        k = len(groups)
+        groups.append(sized)
+        for src, dst, device in copies:
+            pltpu.make_async_remote_copy(
+                src_ref=src, dst_ref=dst, send_sem=ssem.at[k], recv_sem=rsem.at[k],
+                device_id=device, device_id_type=MESH,
+            ).start()
+        return k
+
+    def arrive(*ks):
+        for k in ks:
+            pltpu.make_async_copy(groups[k], groups[k], rsem.at[k]).wait()
 
     barrier = pltpu.get_barrier_semaphore()
     peers = [zp(1), zp(3)] + [pp(d) for d in PLANE] + column
@@ -90,12 +91,13 @@
     pl.semaphore_wait(barrier, len(peers))
 
     def spread(w, src):
-        return [send(src, bg.at[w, x, y], pp(d)) for d in PLANE]
-
-    z_up = [send(bt_hbm.at[0], bg.at[zh, x, y, 0], zp(1))]
-    z_down = [send(bt_hbm.at[1], bg.at[zh, x, y, 1], zp(3))]
-    z_up.append(send(bt_hbm.at[1], bg.at[zh, x, y, 1], zp(1)))
-    z_down.append(send(bt_hbm.at[0], bg.at[zh, x, y, 0], zp(3)))
+        return send([(src, bg.at[w, x, y], pp(d)) for d in PLANE], slots)
+
+    h0, h1 = bg.at[zh, x, y, 0], bg.at[zh, x, y, 1]
+    z_up0 = send([(bt_hbm.at[0], h0, zp(1))], h0)
+    z_down1 = send([(bt_hbm.at[1], h1, zp(3))], h1)
+    z_up1 = send([(bt_hbm.at[1], h1, zp(1))], h1)
+    z_down0 = send([(bt_hbm.at[0], h0, zp(3))], h0)
     own_w = spread(zh, bt_hbm)
 
     loads[3].wait()
@@ -120,26 +122,35 @@
 
     ct_p = permuted(ct)
 
-    a_line = [send(a_hbm, ab.at[zl, core], lp(d, core)) for d in (1, 2, 3)]
-    z_up[0].wait_recv()
+    a_line = send(
+        [(a_hbm, ab.at[zl, core], lp(d, core)) for d in (1, 2, 3)],
+        ab.reshape(8, 16, 256).at[pl.ds(0, 3)],
+    )
+    arrive(z_up0)
     half = bg.at[down, x, y, 0]
-    on_up = send(half, half, zp(1))
-    z_down[0].wait_recv()
+    on_up = send([(half, half, zp(1))], half)
+    arrive(z_down1)
     half = bg.at[up, x, y, 1]
-    on_down = send(half, half, zp(3))
-    z_up[1].wait_recv()
+    on_down = send([(half, half, zp(3))], half)
+    arrive(z_down0)
+    up_1 = send(
+        [(bg.at[up, x, y, 0], bg.at[up, x, y, 0], pp((d, 0))) for d in (2, 1, 3)]
+        + [(bg.at[up, x, y, 1], bg.at[up, x, y, 1], pp((0, d))) for d in (2, 1, 3)],
+        bg.reshape(64, 2, 16, 128).at[pl.ds(0, 3)],
+    )
+    arrive(z_up1)
     down_w = spread(down, bg.at[down, x, y])
-    z_down[1].wait_recv()
-    up_w = spread(up, bg.at[up, x, y])
 
     arrive(a_line)
-    a_twin = send(ab.at[:, core], ab.at[:, core], twin)
+    half = ab.at[:, core]
+    a_twin = send([(half, half, twin)], half)
 
     bg2 = bg.reshape(2048, 128)
 
-    def ordered(w, copies):
-        arrive(copies)
+    def ordered(w, *copies):
+        arrive(*copies)
         rows = pl.ds(pl.multiple_of(w * 64, 64), 64)
+        below = pl.ds(pl.multiple_of(1024 + w * 64, 64), 64)
         for j in range(8):
             for q in range(4):
                 btn[j, pl.ds(w * 64 + q, 16, stride=4), :] = bg2[
@@ -147,12 +158,12 @@
                 ]
         for j in range(8):
             hi, lo = split(btn[j, rows, :])
-            bhi[rows, j * 128 : (j + 1) * 128] = hi
-            blo[rows, j * 128 : (j + 1) * 128] = lo
+            thi[below, j * 128 : (j + 1) * 128] = hi
+            tlo[below, j * 128 : (j + 1) * 128] = lo
 
     ordered(zh, own_w)
 
-    a_twin.wait_recv()
+    arrive(a_twin)
     at[...] = jnp.transpose(ab[...].reshape(128, 256))
     a_t = split(at[...])
     gam[...] = dot3(a_t, a_t, NT)
@@ -165,7 +176,13 @@
                 q * 64 : (q + 1) * 64, i * 128 : (i + 1) * 128
             ]
 
-    arrive([on_up, on_down])
+    arrive(up_1)
+    up_w = send(
+        [(bg.at[up, :, y, 0], bg.at[up, :, y, 0], pp((0, d))) for d in (2, 1, 3)]
+        + [(bg.at[up, x, :, 1], bg.at[up, x, :, 1], pp((d, 0))) for d in (2, 1, 3)],
+        bg.reshape(64, 2, 16, 128).at[pl.ds(0, 12)],
+    )
+    arrive(on_up, on_down)
     far_w = spread(far, bg.at[far, x, y])
 
     for k in range(8):
@@ -175,7 +192,7 @@
 
     for j in range(4):
         cols = slice(j * 256, (j + 1) * 256)
-        got = dot3((whi[...], wlo[...]), (thi[:, cols], tlo[:, cols]), NN)
+        got = dot3((whi[...], wlo[...]), (thi[:1024, cols], tlo[:1024, cols]), NN)
         for i in range(2):
             for q in range(4):
                 gr2[pl.ds((j * 2 + i) * 4 + q, 64, stride=40), :] = got[
@@ -185,25 +202,21 @@
     one, two = pl.ds(0, 2), pl.ds(2, 3)
 
     def scatter1(n, w):
-        return [
-            send(gr.at[w, :, (y + d) % 4, one], r1a.at[n, d - 1], pp((0, d)))
-            for d in (2, 1, 3)
-        ] + [
-            send(gr.at[w, (x + d) % 4, :, two], r1b.at[n, d - 1], pp((d, 0)))
-            for d in (2, 1, 3)
-        ]
+        return send(
+            [(gr.at[w, :, (y + d) % 4, one], r1a.at[n, d - 1], pp((0, d))) for d in (2, 1, 3)]
+            + [(gr.at[w, (x + d) % 4, :, two], r1b.at[n, d - 1], pp((d, 0))) for d in (2, 1, 3)],
+            slots,
+        )
 
     def scatter2(n, w, copies):
         arrive(copies)
         gr[w, :, y, one] = gr[w, :, y, one] + added([r1a[n, i] for i in range(3)])
         gr[w, x, :, two] = gr[w, x, :, two] + added([r1b[n, i] for i in range(3)])
-        return [
-            send(gr.at[w, (x + d) % 4, y, one], r2a.at[n, d - 1], pp((d, 0)))
-            for d in (2, 1, 3)
-        ] + [
-            send(gr.at[w, x, (y + d) % 4, two], r2b.at[n, d - 1], pp((0, d)))
-            for d in (2, 1, 3)
-        ]
+        return send(
+            [(gr.at[w, (x + d) % 4, y, one], r2a.at[n, d - 1], pp((d, 0))) for d in (2, 1, 3)]
+            + [(gr.at[w, x, (y + d) % 4, two], r2b.at[n, d - 1], pp((0, d))) for d in (2, 1, 3)],
+            gr.reshape(64, 5, 8, 128).at[pl.ds(0, 3)],
+        )
 
     def gathered(n, w, copies):
         arrive(copies)
@@ -212,66 +225,60 @@
 
     ordered(down, down_w)
     ordered(up, up_w)
-    pa[...] = jnp.zeros_like(pa)
     arrive(far_w)
     far_s = scatter1(0, far)
-    ordered(far, [])
+    ordered(far)
     up_s = scatter1(1, up)
 
-    b_split = (bhi[...], blo[...])
-    gbm[...] = dot3(b_split, b_split, NT)
-
-    def second(m, _):
-        rows = pl.ds(pl.multiple_of(m * 512, 512), 512)
-        part = dot3((thi[rows, :], tlo[rows, :]), (bhi[...], blo[...]), NT)
-        rows_a = ab[...].reshape(128, 256)
-        acc = pa[...].reshape(128, 256)
-        for k in range(4):
-            one = part[k * 128 : (k + 1) * 128]
-            acc = acc + one * cv[pl.ds(m * 4 + k, 1), :]
-            pck[pl.ds(m * 4 + k, 1), :] = jnp.sum(one * rows_a, axis=0, keepdims=True)
-        pa[...] = acc.reshape(4, 2, 16, 256)
-        return 0
-
-    lax.fori_loop(0, 2, second, 0)
+    b_all = (thi[1024:1280], tlo[1024:1280])
+    rows_a = ab[...].reshape(128, 256)
+    acc = None
+    for m in range(2):
+        rows = slice(m * 640, (m + 1) * 640)
+        part = dot3((thi[rows], tlo[rows]), b_all, NT)
+        for k in range(5 if m == 0 else 3):
+            one_k, at_k = part[k * 128 : (k + 1) * 128], m * 5 + k
+            term = one_k * cv[at_k : at_k + 1]
+            acc = term if acc is None else acc + term
+            pck[at_k : at_k + 1] = jnp.sum(one_k * rows_a, axis=0, keepdims=True)
+    gbm[...] = part[384:]
+    pa[...] = acc.reshape(4, 2, 16, 256)
     cp[here] = dot3(split(cv[...]), split(gam[...] * gbm[...]), NN) - pck[...]
-    c1 = [send(cp.at[here], cp.at[here], pp(d)) for d in PLANE]
-
-    down_s = scatter1(2, down)
+    c1 = send([(cp.at[here], cp.at[here], pp(d)) for d in PLANE], cp.at[pl.ds(0, 15)])
 
     h = split(gbm[...] * gcm[...])
     got = dot3(split(ab[...].reshape(128, 256)), h, NN) - pa[...].reshape(128, 256)
     pa[...] = got.reshape(4, 2, 16, 256)
-    p1 = send(pa.at[:, other], pcore, twin)
+    p1 = send([(pa.at[:, other], pcore, twin)], pcore)
 
     far_s = scatter2(0, far, far_s)
-    up_s = scatter2(1, up, up_s)
+    down_s = scatter1(2, down)
 
     arrive(c1)
     cz[col] = added([cp[i] for i in range(16)])
-    c2 = [send(cz.at[col], cz.at[col], device) for device in column]
+    c2 = send([(cz.at[col], cz.at[col], device) for device in column], cz.at[pl.ds(0, 7)])
+    gathered(0, far, far_s)
+    f_up = send([(gr.at[far, x, y, one], z1a, zp(1))], z1a)
+    f_down = send([(gr.at[far, x, y, two], z1b, zp(3))], z1b)
+
+    arrive(p1)
+    psum[...] = pa[:, core] + pcore[...]
+    p2 = send([(psum.at[(zl + d) % 4], pz.at[d - 1], lp(d, core)) for d in (1, 2, 3)], pz)
+    up_s = scatter2(1, up, up_s)
     down_s = scatter2(2, down, down_s)
-    gathered(0, far, far_s)
-    f_up = send(gr.at[far, x, y, one], z1a, zp(1))
-    f_down = send(gr.at[far, x, y, two], z1b, zp(3))
     own_s = scatter1(3, zh)
-
-    p1.wait_recv()
-    psum[...] = pa[:, core] + pcore[...]
-    p2 = [send(psum.at[(zl + d) % 4], pz.at[d - 1], lp(d, core)) for d in (1, 2, 3)]
-    gathered(1, up, up_s)
-    gathered(2, down, down_s)
 
     arrive(c2)
     ch[zh] = added([cz[i] for i in range(8)])
-    c3 = [send(ch.at[zh], ch.at[zh], zp(d)) for d in (2, 1, 3)]
-
-    f_up.wait_recv()
+    c3 = send([(ch.at[zh], ch.at[zh], zp(d)) for d in (2, 1, 3)], ch.at[pl.ds(0, 3)])
+    gathered(1, up, up_s)
+    arrive(f_up)
     gr[up, x, y, one] = gr[up, x, y, one] + z1a[...]
-    l_up = send(gr.at[up, x, y], z2.at[0], zp(1))
-    f_down.wait_recv()
+    l_up = send([(gr.at[up, x, y], z2.at[0], zp(1))], z2.at[0])
+    gathered(2, down, down_s)
+    arrive(f_down)
     gr[down, x, y, two] = gr[down, x, y, two] + z1b[...]
-    l_down = send(gr.at[down, x, y], z2.at[1], zp(3))
+    l_down = send([(gr.at[down, x, y], z2.at[1], zp(3))], z2.at[1])
     own_s = scatter2(3, zh, own_s)
 
     arrive(p2)
@@ -283,12 +290,12 @@
     stores[0].start()
     gathered(3, zh, own_s)
 
-    arrive([l_up, l_down])
+    arrive(l_up, l_down)
     got = gr[zh, x, y] + z2[0] + z2[1]
     gram_a = jnp.concatenate([got[4, :4], got[4, 4:]], 1)
     gram_c = jnp.concatenate([gcm[pl.ds(row * 4 + q, 1), :] for q in range(4)], 0)
     h = jnp.concatenate([gram_a * gram_c, jnp.zeros((12, 256), F32)], 0)
-    h = dot3(split(h), (bhi[...], blo[...]), NN)[:4]
+    h = dot3(split(h), (thi[1024:1280], tlo[1024:1280]), NN)[:4]
     for t in range(4):
         two = [h[:, (2 * t + i) * 128 : (2 * t + i + 1) * 128] for i in range(2)]
         gbt_out[t] = jnp.concatenate(two, 0) - got[t]
@@ -296,8 +303,8 @@
     arrive(c3)
     gc_out[...] = added([ch[i] for i in range(4)])
     stores[2].start()
-    for copy in sent:
-        copy.wait_send()
+    for k, sized in enumerate(groups):
+        pltpu.make_async_copy(sized, sized, ssem.at[k]).wait()
     for store in stores:
         store.wait()
 
@@ -323,15 +330,13 @@
         out_specs=(pl.BlockSpec(memory_space=pl.ANY),) * 3,
         scratch_shapes=[
             pltpu.VMEM((8, 128, 1024), F32),
-            pltpu.VMEM((1024, 1024), BF16),
-            pltpu.VMEM((1024, 1024), BF16),
+            pltpu.VMEM((1280, 1024), BF16),
+            pltpu.VMEM((1280, 1024), BF16),
             pltpu.VMEM((256, 1024), BF16),
             pltpu.VMEM((256, 1024), BF16),
             pltpu.VMEM((4, 2, 16, 256), F32),
             pltpu.VMEM((4, 4, 4, 2, 16, 128), F32),
             pltpu.VMEM((8, 256, 128), F32),
-            pltpu.VMEM((256, 1024), BF16),
-            pltpu.VMEM((256, 1024), BF16),
             pltpu.VMEM((256, 256), F32),
             pltpu.VMEM((256, 256), F32),
             pltpu.VMEM((256, 256), F32),

time: 53.9 us -> 51.6 us (0.957)
  Pallas kernels: 53.2 us -> 50.5 us
    pallas_call x1, Pallas kernels: 52.5 us -> 49.9 us  [local(): pl.pallas_call(kernel, out_shape=tuple((pltpu.VMEM(v.shape, v.dtype) for...]
where the time goes in v4:
time: 51.6 us; the launch traced here: 51.1 us
  Pallas kernels  50.5 us (98%)
  between operations  0.64 us (1%)
    pallas_call x1, Pallas kernels, local(): pl.pallas_call(kernel, out_shape=tuple((pltpu.VMEM(v.shape, v.dtype) for...  49.9 us

profile of v4, /device:TPU:1, one launch (start us, length us, event | category | flops | bytes accessed | tf_op | source)
XLA Modules:
  0.0 51.1 jit_solution(8279313529177290419)
XLA Ops:
  0.6 49.9 %shard_map.67 = (f32[16,256]{1,0:T(8,128)S(1)}, f32[4,8,128]{2,1,0:T(8,128)S(1)}, f32[8,256]{1,0:T(8,128)S(1)}) custom-call(f32[8,128,1024]{2,1,0:T(8,128)} %t_hbm.1, f32[16,256]{1,0:T(8,128)} %a_hbm.1, f32[2,16,128]{2,1,0:T(8,128)} %bitcast.10, f32[8,256]{1,0:T(8,128)} %c_hbm.1), custom_call_target="tpu_custom_call" | custom-call | tf_op jit(solution)/shard_map/pallas_call | solution.py:326
  50.5 0.6 %shard_map.68 = (f32[16,256]{1,0:T(8,128)}, f32[4,8,128]{2,1,0:T(8,128)}, f32[8,256]{1,0:T(8,128)}) custom-call(f32[16,256]{1,0:T(8,128)S(1)} %get-tuple-element.9.a_in, f32[4,8,128]{2,1,0:T(8,128)S(1)} %get-tuple-element.10.b_in, f32[8,256]{1,0:T(8,128)S(1)} %get-tuple-element.11.c_in), custom_call_target="tpu_custom_call" | custom-call | tf_op jit(solution)/shard_map/pallas_call | solution.py:371

commit v5 on v4

--- a/solution.py
+++ b/solution.py
@@ -201,34 +201,40 @@
 
     one, two = pl.ds(0, 2), pl.ds(2, 3)
 
+    def parts_of(n):
+        first, second = (one, r1a, r2a), (two, r1b, r2b)
+        return (first, second) if n % 2 == 0 else (second, first)
+
     def scatter1(n, w):
+        (ty, y1, _), (tx, x1, _) = parts_of(n)
         return send(
-            [(gr.at[w, :, (y + d) % 4, one], r1a.at[n, d - 1], pp((0, d))) for d in (2, 1, 3)]
-            + [(gr.at[w, (x + d) % 4, :, two], r1b.at[n, d - 1], pp((d, 0))) for d in (2, 1, 3)],
+            [(gr.at[w, :, (y + d) % 4, ty], y1.at[n, d - 1], pp((0, d))) for d in (2, 1, 3)]
+            + [(gr.at[w, (x + d) % 4, :, tx], x1.at[n, d - 1], pp((d, 0))) for d in (2, 1, 3)],
             slots,
         )
 
     def scatter2(n, w, copies):
         arrive(copies)
-        gr[w, :, y, one] = gr[w, :, y, one] + added([r1a[n, i] for i in range(3)])
-        gr[w, x, :, two] = gr[w, x, :, two] + added([r1b[n, i] for i in range(3)])
+        (ty, y1, y2), (tx, x1, x2) = parts_of(n)
+        gr[w, :, y, ty] = gr[w, :, y, ty] + added([y1[n, i] for i in range(3)])
+        gr[w, x, :, tx] = gr[w, x, :, tx] + added([x1[n, i] for i in range(3)])
         return send(
-            [(gr.at[w, (x + d) % 4, y, one], r2a.at[n, d - 1], pp((d, 0))) for d in (2, 1, 3)]
-            + [(gr.at[w, x, (y + d) % 4, two], r2b.at[n, d - 1], pp((0, d))) for d in (2, 1, 3)],
+            [(gr.at[w, (x + d) % 4, y, ty], y2.at[n, d - 1], pp((d, 0))) for d in (2, 1, 3)]
+            + [(gr.at[w, x, (y + d) % 4, tx], x2.at[n, d - 1], pp((0, d))) for d in (2, 1, 3)],
             gr.reshape(64, 5, 8, 128).at[pl.ds(0, 3)],
         )
 
     def gathered(n, w, copies):
         arrive(copies)
-        gr[w, x, y, one] = gr[w, x, y, one] + added([r2a[n, i] for i in range(3)])
-        gr[w, x, y, two] = gr[w, x, y, two] + added([r2b[n, i] for i in range(3)])
+        (ty, _, y2), (tx, _, x2) = parts_of(n)
+        gr[w, x, y, ty] = gr[w, x, y, ty] + added([y2[n, i] for i in range(3)])
+        gr[w, x, y, tx] = gr[w, x, y, tx] + added([x2[n, i] for i in range(3)])
 
     ordered(down, down_w)
     ordered(up, up_w)
     arrive(far_w)
     far_s = scatter1(0, far)
     ordered(far)
-    up_s = scatter1(1, up)
 
     b_all = (thi[1024:1280], tlo[1024:1280])
     rows_a = ab[...].reshape(128, 256)
@@ -252,6 +258,7 @@
     p1 = send([(pa.at[:, other], pcore, twin)], pcore)
 
     far_s = scatter2(0, far, far_s)
+    up_s = scatter1(1, up)
     down_s = scatter1(2, down)
 
     arrive(c1)

time: 51.6 us -> 50.6 us (0.981)
  Pallas kernels: 50.5 us -> 49.6 us
    pallas_call x1, Pallas kernels: 49.9 us -> 49 us  [local(): pl.pallas_call(kernel, out_shape=tuple((pltpu.VMEM(v.shape, v.dtype) for...]
where the time goes in v5:
time: 50.6 us; the launch traced here: 50.2 us
  Pallas kernels  49.6 us (98%)
  between operations  0.64 us (1%)
    pallas_call x1, Pallas kernels, local(): pl.pallas_call(kernel, out_shape=tuple((pltpu.VMEM(v.shape, v.dtype) for...  49 us

profile of v5, /device:TPU:1, one launch (start us, length us, event | category | flops | bytes accessed | tf_op | source)
XLA Modules:
  0.0 50.2 jit_solution(12934882810051625394)
XLA Ops:
  0.6 49.0 %shard_map.67 = (f32[16,256]{1,0:T(8,128)S(1)}, f32[4,8,128]{2,1,0:T(8,128)S(1)}, f32[8,256]{1,0:T(8,128)S(1)}) custom-call(f32[8,128,1024]{2,1,0:T(8,128)} %t_hbm.1, f32[16,256]{1,0:T(8,128)} %a_hbm.1, f32[2,16,128]{2,1,0:T(8,128)} %bitcast.10, f32[8,256]{1,0:T(8,128)} %c_hbm.1), custom_call_target="tpu_custom_call" | custom-call | tf_op jit(solution)/shard_map/pallas_call | solution.py:333
  49.6 0.6 %shard_map.68 = (f32[16,256]{1,0:T(8,128)}, f32[4,8,128]{2,1,0:T(8,128)}, f32[8,256]{1,0:T(8,128)}) custom-call(f32[16,256]{1,0:T(8,128)S(1)} %get-tuple-element.9.a_in, f32[4,8,128]{2,1,0:T(8,128)S(1)} %get-tuple-element.10.b_in, f32[8,256]{1,0:T(8,128)S(1)} %get-tuple-element.11.c_in), custom_call_target="tpu_custom_call" | custom-call | tf_op jit(solution)/shard_map/pallas_call | solution.py:378
